TPU v7x, 256 devices: a whole 4x4x8 slice. The times are simulated.
256 devices in a mesh: shell: 8 (over z), sector: 32 (over x, y, core).
Axes of the slice: x: 4, y: 4, z: 8, core: 2. Of those that a mesh axis runs over, the one named last changes fastest.
Arguments:
- bricks: bfloat16 [8, 256, 32, 512], P('shell', 'sector'), may hold values from -6 to 6
- conv_w: bfloat16 [32, 864], replicated, may hold values from -0.21875 to 0.21875
- conv_b: float32 [32], replicated, may hold values from -3 to 3
- head_w1: bfloat16 [32, 64], replicated, may hold values from -1 to 1
- head_b1: float32 [64], replicated, may hold values from -3 to 3
- head_w2: float32 [64, 2], replicated, may hold values from -0.75 to 0.75
- queries: int32 [8, 1024, 256], P('shell', 'sector'), may hold values from -1 to 4095, as said below
- sample_src: int32 [8, 131072], P('shell', 'sector'), may hold values from 0 to 8191, as said below
- depth_target: float32 [16384], P('sector'), may hold values from 0.1 to 0.9
- inten_target: float32 [16384], P('sector'), may hold values from 0 to 1
- drop_label: int32 [16384], P('sector'), may hold values 0 or 1
Outputs:
- loss_mean: float32 [], replicated
- grad_conv_w: float32 [32, 864], replicated
- grad_conv_b: float32 [32], replicated
- grad_head_w1: float32 [32, 64], replicated
- grad_head_b1: float32 [64], replicated
- grad_head_w2: float32 [64, 2], replicated
- grad_bricks: bfloat16 [8, 256, 32, 512], P('shell', 'sector')
- ray_depth: float32 [16384], P('sector')
Inputs may be any that keep to these rules, and one draw needn't show every extreme that they name: `queries`: entry of the buffer from a device of sector v to owner w: a cell address (brick of the owner times 512 plus cell) or -1 for an empty slot. Every sample of a device holds exactly one live slot, named by sample_src as w * 256 + slot. In every shell one owner receives full buffers of 256 from every sector. `sample_src`: A slot w * 256 + slot of the sample's own device; distinct samples of a device have distinct slots.
All inputs are finite; a program needn't handle non-finite values. No bound on the sum of `drop_label` on one device may be relied on, other than what follows from the above.
Results may differ from a plain program's by a relative error of at most 0.0015.
The roundings to bfloat16 on the way count: a program that leaves them out, or rounds other values in their place, can miss the bound.
Values may be sent and summed in bfloat16 or wider, within the bound.
No kernel may reach another device: no remote copies, remote signals or barrier semaphores. Data moves between devices by JAX's collectives and lax.ppermute only.
A program may use at most 192 MiB of HBM per device.

v0:
```python
import math
import jax
import jax.numpy as jnp
from jax import lax
from jax.sharding import PartitionSpec as P

SAMP = 8
HIGHEST = lax.Precision.HIGHEST
CUBE_OFFSETS = [(a, b, c) for a in range(3) for b in range(3) for c in range(3)]


def entering(value, axis, join, neutral, backward):
    count, mine = (lax.axis_size(axis), lax.axis_index(axis))
    pieces = lax.all_gather(value, axis)
    if backward:
        pieces = pieces[::-1]
        mine = count - 1 - mine
    total = jnp.full_like(value, 0) + jnp.asarray(neutral, value.dtype)

    def hop(position, total):
        longer = join(total, pieces[position])
        return jnp.where(position < mine, longer, total)

    return lax.fori_loop(0, count - 1, hop, total)


def unfold_cells(block_set):
    brick_count = block_set.shape[0]
    channel_width = block_set.shape[1]
    cube = block_set.reshape(brick_count, channel_width, 8, 8, 8)
    padded = jnp.pad(cube, ((0, 0), (0, 0), (1, 1), (1, 1), (1, 1)))
    columns = [
        padded[:, :, a : a + 8, b : b + 8, c : c + 8].reshape(brick_count, channel_width, 512)
        for a, b, c in CUBE_OFFSETS
    ]
    return jnp.stack(columns, axis=1).reshape(brick_count, 27 * channel_width, 512)


def conv_backward(block_set, block_cot, conv_w, conv_b):
    unfolded = unfold_cells(block_set)
    pre_act = (
        jnp.einsum("oc,bcn->obn", conv_w, unfolded, preferred_element_type=jnp.float32)
        + conv_b[:, None, None]
    )
    _, gelu_pull = jax.vjp(jax.nn.gelu, pre_act)
    pre_grad = gelu_pull(block_cot)[0].astype(jnp.bfloat16)
    weight_grad = jnp.einsum("obn,bcn->oc", pre_grad, unfolded, preferred_element_type=jnp.float32)
    bias_grad = jnp.sum(pre_grad.astype(jnp.float32), axis=(1, 2))
    column_grad = jnp.einsum("oc,obn->bcn", conv_w, pre_grad, preferred_element_type=jnp.float32)
    _, fold_pull = jax.vjp(unfold_cells, jnp.zeros(block_set.shape, jnp.float32))
    block_grad = fold_pull(column_grad)[0]
    return (weight_grad, bias_grad, block_grad.astype(jnp.bfloat16))


def field_head(feature_cols, weight_one, bias_one, weight_two):
    hidden = (
        jnp.einsum("ch,cm->hm", weight_one, feature_cols, precision=HIGHEST) + bias_one[:, None]
    )
    outputs = jnp.einsum("hk,hm->km", weight_two, jax.nn.gelu(hidden), precision=HIGHEST)
    return (jax.nn.softplus(outputs[0]), jax.nn.sigmoid(outputs[1]))


def render_terms(density, intensity, depth_grid, step_size):
    optical = density * step_size
    before = jnp.cumsum(optical, axis=-1) - optical
    weights = jnp.exp(-before) * (1.0 - jnp.exp(-optical))
    return (
        jnp.sum(weights * depth_grid, axis=-1),
        jnp.sum(weights * intensity, axis=-1),
        jnp.sum(optical, axis=-1),
    )


def add_terms(first_term, second_term):
    return first_term + second_term


def local(
    bricks,
    conv_w,
    conv_b,
    head_w1,
    head_b1,
    head_w2,
    queries,
    sample_src,
    depth_target,
    inten_target,
    drop_label,
):
    shells = lax.axis_size("shell")
    sectors = lax.axis_size("sector")
    shell_index = lax.axis_index("shell")
    local_bricks = bricks[0]
    brick_count = local_bricks.shape[0]
    channels = local_bricks.shape[1]
    group_size = math.gcd(brick_count, 8)
    group_cols = group_size * 512
    group_total = brick_count // group_size
    weight_one = head_w1.astype(jnp.float32)
    brick_groups = local_bricks.reshape(group_total, group_size, channels, 512)

    def decode_group(group_id, table_now):
        block_set = lax.dynamic_index_in_dim(brick_groups, group_id, 0, keepdims=False)
        pre_act = (
            jnp.einsum(
                "oc,bcn->obn", conv_w, unfold_cells(block_set), preferred_element_type=jnp.float32
            )
            + conv_b[:, None, None]
        )
        values = jax.nn.gelu(pre_act).astype(jnp.bfloat16).reshape(channels, group_cols)
        return values

    cell_table = lax.fori_loop(
        0, group_total, decode_group, jnp.zeros((channels, brick_count * 512), jnp.bfloat16)
    )
    requests = queries[0]
    capacity = requests.shape[1]
    owner_addr = lax.all_to_all(
        requests, "sector", split_axis=0, concat_axis=0, tiled=True
    ).reshape(-1)
    live_slot = owner_addr >= 0
    picked = jnp.take(cell_table, jnp.where(live_slot, owner_addr, 0), axis=1)
    owner_feats = jnp.where(live_slot[None, :], picked, jnp.zeros((), jnp.bfloat16))
    sources = sample_src[0]
    replies = lax.all_to_all(
        owner_feats.reshape(channels, sectors, capacity),
        "sector",
        split_axis=1,
        concat_axis=1,
        tiled=True,
    )
    sample_cols = jnp.take(replies.reshape(channels, sectors * capacity), sources, axis=1).astype(
        jnp.float32
    )
    (density, intensity), head_pull = jax.vjp(field_head, sample_cols, weight_one, head_b1, head_w2)
    ray_count = sources.shape[0] // SAMP
    density = density.reshape(ray_count, SAMP)
    intensity = intensity.reshape(ray_count, SAMP)
    step_size = 2.0 / (shells * SAMP)
    depth_grid = (
        shell_index.astype(jnp.float32) * SAMP + jnp.arange(SAMP, dtype=jnp.float32) + 0.5
    ) / (shells * SAMP)

    def local_render(dens_in, inten_in):
        return render_terms(dens_in, inten_in, depth_grid, step_size)

    (shell_depth, shell_inten, shell_tau), render_pull = jax.vjp(local_render, density, intensity)
    dropped = drop_label.astype(jnp.float32)
    kept_weight = 1.0 - dropped
    zeros_rays = jnp.zeros_like(shell_tau)
    prefix = entering(shell_tau, "shell", add_terms, zeros_rays, False)
    entry_trans = jnp.exp(-prefix)
    ray_depth, ray_inten, tau_total = lax.psum(
        (entry_trans * shell_depth, entry_trans * shell_inten, shell_tau), "shell"
    )
    escape = jnp.exp(-tau_total)
    grad_depth = 2.0 * kept_weight * (ray_depth - depth_target)
    grad_inten = 2.0 * kept_weight * (ray_inten - inten_target)
    own_weight = (grad_depth * shell_depth + grad_inten * shell_inten) * entry_trans
    behind = entering(own_weight, "shell", add_terms, zeros_rays, True)
    grad_escape = 2.0 * (escape - dropped)
    dens_grad, inten_grad = render_pull(
        (grad_depth * entry_trans, grad_inten * entry_trans, -grad_escape * escape - behind)
    )
    ray_loss = jnp.sum(
        kept_weight * ((ray_depth - depth_target) ** 2 + (ray_inten - inten_target) ** 2)
        + (escape - dropped) ** 2
    )
    loss_mean = lax.psum(ray_loss, "sector") / (ray_count * sectors)
    sample_grad, grad_one, grad_bias_one, grad_two = head_pull(
        (dens_grad.reshape(-1), inten_grad.reshape(-1))
    )
    buckets = jnp.zeros((channels, sectors * capacity), jnp.float32).at[:, sources].set(sample_grad)
    owner_grad = lax.all_to_all(
        buckets.reshape(channels, sectors, capacity),
        "sector",
        split_axis=1,
        concat_axis=1,
        tiled=True,
    ).reshape(channels, sectors * capacity)
    target_index = jnp.where(live_slot, owner_addr, brick_count * 512)
    table_grad = (
        jnp.zeros((channels, brick_count * 512), jnp.float32)
        .at[:, target_index]
        .add(owner_grad, mode="drop")
    )

    def conv_back(totals, group_id):
        block_set = lax.dynamic_index_in_dim(brick_groups, group_id, 0, keepdims=False)
        block_cot = table_grad.reshape(channels, group_size, 512)
        weight_grad, bias_grad, block_grad = conv_backward(block_set, block_cot, conv_w, conv_b)
        return ((totals[0] + weight_grad, totals[1] + bias_grad), block_grad)

    start = (jnp.zeros(conv_w.shape, jnp.float32), jnp.zeros_like(conv_b))
    (conv_grad, conv_bias_grad), brick_grads = lax.scan(
        conv_back, start, jnp.arange(group_total, dtype=jnp.int32)
    )
    summed = lax.psum(
        (conv_grad, conv_bias_grad, grad_one, grad_bias_one, grad_two), ("shell", "sector")
    )
    return (
        loss_mean,
        summed[0],
        summed[1],
        summed[2],
        summed[3],
        summed[4],
        brick_grads,
        ray_depth,
    )


def solution(mesh):
    return jax.shard_map(
        local,
        mesh=mesh,
        in_specs=(
            P("shell", "sector", None, None),
            P(),
            P(),
            P(),
            P(),
            P(),
            P("shell", "sector", None),
            P("shell", "sector"),
            P("sector"),
            P("sector"),
            P("sector"),
        ),
        out_specs=(P(), P(), P(), P(), P(), P(), P("shell", "sector", None, None), P("sector")),
        check_vma=False,
    )
```

profile of v0, /device:TPU:1, one launch (start us, length us, event | category | flops | bytes accessed | tf_op | source)
XLA Modules:
  0.0 665.0 jit_solution(13087959850178110753)
XLA Ops:
  8.6 8.6 %all-to-all-start = ((s32[32,1,256]{2,1,0:T(1,128)}), s32[32,1,256]{2,1,0:T(1,128)S(1)}, u32[]{:S(2)}, u32[]{:S(2)}) async-start(s32[32,1,256]{2,1,0:T(1,128)} %all_to_all.12), calls=%async_computation | async-start | bytes 65536 | tf_op jit(solution)/shard_map/all_to_all | solution.py:119
  18.6 3.4 pad_slice_fusion.1
  22.1 6.8 %pad_slice_fusion = (bf16[8,32,8,8,8]{1,4,3,2,0:T(8,128)(2,1)}, bf16[8,32,8,8,8]{1,4,3,2,0:T(8,128)(2,1)}, bf16[8,32,8,8,8]{1,4,3,2,0:T(8,128)(2,1)}, bf16[8,32,...) fusion(bf16[8,32,8,8,8]{1,4,3,2,0:T(8,128)(2,1)S(1)} %bitcast.139), kind=kLoop, calls=%fused_computation.8 | loop fusion | bytes 5242880 | tf_op jit(solution)/shard_map/while/body/eval_jaxpr/slice | solution.py:33
  118.1 5.1 multiply_convert_fusion
  124.4 24.0 %gather_fusion = bf16[8192,32]{1,0:T(8,128)(2,1)S(1)} fusion(bf16[32,4096]{0,1:T(8,128)(2,1)S(1)} %bitcast.136, s32[8192]{0:T(1024)S(1)} %broadcast_clamp_fusion), kind=kCustom, calls=%fused_computation | custom fusion | bytes 1081344 | tf_op jit(solution)/shard_map/jit(_take)/gather | solution.py:123
  150.3 7.4 %all-to-all-start.1 = ((bf16[32,32,256]{2,0,1:T(8,128)(2,1)}), bf16[32,32,256]{2,0,1:T(8,128)(2,1)S(1)}, u32[]{:S(2)}, u32[]{:S(2)}) async-start(bf16[32,32,256]{2,0,1:T(8,128)(2,1)} %select_select_fusion), calls=%async_computation.1 | async-start | bytes 1048576 | tf_op jit(solution)/shard_map/all_to_all | solution.py:126
  157.8 11.5 %all-to-all-done.1 = bf16[32,32,256]{2,0,1:T(8,128)(2,1)S(1)} async-done(((bf16[32,32,256]{2,0,1:T(8,128)(2,1)}), bf16[32,32,256]{2,0,1:T(8,128)(2,1)S(1)}, u32[]{:S(2)}, u32[]{:S(2)}) %all-to-all-start.1) | async-done | bytes 524320 | tf_op jit(solution)/shard_map/all_to_all | solution.py:126
  170.4 12.1 %gather_fusion.1 = bf16[4096,32]{1,0:T(8,128)(2,1)S(1)} fusion(bf16[32,8192]{0,1:T(8,128)(2,1)S(1)} %bitcast.163, s32[4096]{0:T(1024)S(1)} %broadcast_clamp_fusion.1), kind=kCustom, calls=%fused_computation.1 | custom fusion | bytes 540672 | tf_op jit(solution)/shard_map/jit(_take)/gather | solution.py:133
  187.0 19.6 %all-gather.2 = f32[8,1,512]{2,1,0:T(1,128)S(1)} all-gather(f32[1,1,512]{2,1,0:T(1,128)S(1)} %bitcast.209), channel_id=2, replica_groups=mesh['shell'=8,'sector'=32] {'shell'}, dimensions={0}, use_global_device_ids=true | all-gather | bytes 18432 | tf_op jit(solution)/shard_map/all_gather | solution.py:14
  207.0 11.4 %all-reduce.31 = (f32[512]{0:T(512)S(1)}, f32[512]{0:T(512)S(1)}, f32[512]{0:T(512)S(1)}) all-reduce(f32[512]{0:T(512)S(1)} %get-tuple-element.265, f32[512]{0:T(512)S(1)} %get-tuple-element.360, f32[512]{0:T(512)S(1)} %get-tuple-element.359), channel_id=1, replica_groups=mesh['shell'=8,'sector'=32] {'shell'}, use_global_device_ids=true, to_apply=%region_8.9 | all-reduce | flops 1536 | bytes 12288 | tf_op jit(solution)/shard_map/psum | solution.py:154
  220.8 15.9 %all-gather.3 = f32[8,1,512]{2,1,0:T(1,128)S(1)} all-gather(f32[1,1,512]{2,1,0:T(1,128)} %bitcast.210), channel_id=3, replica_groups=mesh['shell'=8,'sector'=32] {'shell'}, dimensions={0}, use_global_device_ids=true | all-gather | bytes 18432 | tf_op jit(solution)/shard_map/all_gather | solution.py:14
  239.9 2.4 fusion.56
  242.3 3.9 fusion.57
  246.2 13.2 %scatter_custom_fusion = f32[32,8192]{0,1:T(8,128)} fusion(s32[4096]{0:T(1024)S(1)} %bitcast.205, f32[4096,32]{1,0:T(8,128)} %fusion.57, f32[]{:T(128)} %constant.164.clone.1), kind=kCustom, calls=%fused_computation.45 | custom fusion | bytes 1049088 | tf_op jit(solution)/shard_map/scatter | solution.py:174
  259.5 3.6 copy.154
  263.1 18.7 %all-to-all-start.2 = ((f32[32,32,256]{2,0,1:T(8,128)}), f32[32,32,256]{2,0,1:T(8,128)S(1)}, u32[]{:S(2)}, u32[]{:S(2)}) async-start(f32[32,32,256]{2,0,1:T(8,128)} %copy.154), calls=%async_computation.2 | async-start | bytes 2097152 | tf_op jit(solution)/shard_map/all_to_all | solution.py:175
  281.8 71.8 %psum.66 = f32[]{:T(128)} all-reduce(f32[]{:T(128)} %get-tuple-element.354), channel_id=1, replica_groups=mesh['shell'=8,'sector'=32] {'sector'}, use_global_device_ids=true, to_apply=%region_10.11 | all-reduce | flops 1 | bytes 8 | tf_op jit(solution)/shard_map/psum | solution.py:170
  358.3 2.8 copy.156
  361.1 45.0 %scatter_custom_fusion.1 = f32[32,4096]{0,1:T(8,128)S(1)} fusion(s32[8192]{0:T(1024)} %bitcast.208, f32[8192,32]{1,0:T(8,128)} %copy.156, f32[]{:T(128)} %constant.164.clone.1), kind=kCustom, calls=%fused_computation.58 | custom fusion | flops 262144 | bytes 524800 | tf_op jit(solution)/shard_map/scatter-add | solution.py:186
  407.2 5.8 convolution_bitcast_fusion.2
  417.1 3.4 fusion.54
  422.1 3.0 copy.197
  425.1 3.0 copy.204
  428.1 3.0 copy.203
  431.0 3.0 copy.202
  434.0 3.0 copy.201
  437.0 3.0 copy.200
  440.0 3.0 copy.199
  443.0 3.0 copy.223
  445.9 3.0 copy.222
  448.9 3.0 copy.221
  451.9 3.0 copy.220
  454.9 3.0 copy.219
  457.9 3.0 copy.218
  460.9 3.0 copy.217
  463.9 3.0 copy.216
  466.9 3.0 copy.215
  469.8 3.0 copy.214
  472.8 3.0 copy.213
  475.9 3.0 copy.212
  478.8 3.0 copy.211
  481.8 3.0 copy.210
  484.8 3.0 copy.209
  487.8 3.0 copy.208
  490.8 3.2 copy.207
  497.9 16.8 %pad_add_fusion = f32[8,32,10,10,10]{1,4,3,2,0:T(8,128)S(1)} fusion(f32[8,32,8,8,8]{1,4,3,2,0:T(8,128)} %bitcast.148, f32[8,32,8,8,8]{1,4,3,2,0:T(8,128)} %bitcast.149, f32[8,32,8,8,8]{1,4,3,2,0:T(8,128)} %bitcast.150, f32[8,32,8,8,8]{1,4,3,2,0:T(8,128)} %bitcast.151, f32[8,32,8,8,8]{1,4,3,2,0:T(8,128)} %bitcast.152, f32[8,32,8,8,8]{1,4,3,2,0:T(8,128)} %bitcast.153, ...), kind=kLoop, calls=%fused_computation.34 | loop fusion | flops 5376000 | bytes 12558336 | tf_op jit(solution)/shard_map/while/body/eval_jaxpr/transpose(jvp())/add_any | solution.py:33
  515.8 72.8 %all-reduce.30 = (f32[32]{0:T(128)}, f32[32,64]{1,0:T(8,128)}, f32[64]{0:T(128)}, f32[64,2]{0,1:T(2,128)}) all-reduce(f32[32]{0:T(128)S(1)} %get-tuple-element.289, f32[32,64]{1,0:T(8,128)S(1)} %fusion.21, f32[64]{0:T(128)S(1)} %get-tuple-element.363, f32[64,2]{0,1:T(2,128)S(1)} %fusion.20), channel_id=1, replica_groups=mesh['shell'=8,'sector'=32] {'shell','sector'}, use_global_device_ids=true, to_apply=%region_18.19 | all-reduce | flops 2272 | bytes 18176 | tf_op jit(solution)/shard_map/psum | solution.py:199
  589.7 65.3 %all-reduce.34.cloned.1.call-done = f32[32,864]{1,0:T(8,128)} async-done(((f32[32,864]{1,0:T(8,128)}), f32[32,864]{1,0:T(8,128)}) %all-reduce.34.cloned.1.call-update) | async-done | bytes 110608 | tf_op jit(solution)/shard_map/psum | solution.py:199
  (200 shorter events, 125.2 us)
Async XLA Ops:
  7.2 110.9 %copy-start = (bf16[32,864]{1,0:T(8,128)(2,1)S(1)}, bf16[32,864]{1,0:T(8,128)(2,1)}, u32[]{:S(2)}) copy-start(bf16[32,864]{1,0:T(8,128)(2,1)} %param.16) | copy-start | bytes 165892
  8.6 115.1 %all-to-all-start = ((s32[32,1,256]{2,1,0:T(1,128)}), s32[32,1,256]{2,1,0:T(1,128)S(1)}, u32[]{:S(2)}, u32[]{:S(2)}) async-start(s32[32,1,256]{2,1,0:T(1,128)} %all_to_all.12), calls=%async_computation | async-start | bytes 65536 | tf_op jit(solution)/shard_map/all_to_all | solution.py:119
  22.1 6.8 %copy-start.18 = (s32[1,4096]{1,0:T(1,128)S(1)}, s32[1,4096]{1,0:T(1,128)}, u32[]{:S(2)}) copy-start(s32[1,4096]{1,0:T(1,128)} %param.22) | copy-start | bytes 49156
  28.9 13.6 %copy-start.9 = (bf16[8,32,8,8,8]{1,4,3,2,0:T(8,128)(2,1)S(1)}, bf16[8,32,8,8,8]{1,4,3,2,0:T(8,128)(2,1)}, u32[]{:S(2)}) copy-start(bf16[8,32,8,8,8]{1,4,3,2,0:T(8,128)(2,1)} %get-tuple-element.345) | copy-start | bytes 786436
  43.6 22.6 %copy-start.8 = (bf16[8,32,8,8,8]{1,4,3,2,0:T(8,128)(2,1)S(1)}, bf16[8,32,8,8,8]{1,4,3,2,0:T(8,128)(2,1)}, u32[]{:S(2)}) copy-start(bf16[8,32,8,8,8]{1,4,3,2,0:T(8,128)(2,1)} %get-tuple-element.330) | copy-start | bytes 786436
  61.7 30.3 %copy-start.12 = (bf16[1,8,32,512]{3,2,1,0:T(8,128)(2,1)S(1)}, bf16[1,8,32,512]{3,2,1,0:T(8,128)(2,1)}, u32[]{:S(2)}) copy-start(bf16[1,8,32,512]{3,2,1,0:T(8,128)(2,1)} %param.15) | copy-start | bytes 786436
  67.2 32.2 %copy-start.7 = (bf16[8,32,8,8,8]{1,4,3,2,0:T(8,128)(2,1)S(1)}, bf16[8,32,8,8,8]{1,4,3,2,0:T(8,128)(2,1)}, u32[]{:S(2)}) copy-start(bf16[8,32,8,8,8]{1,4,3,2,0:T(8,128)(2,1)} %get-tuple-element.336) | copy-start | bytes 786436
  92.7 23.9 %copy-start.13 = (bf16[8,1,32,512]{3,2,1,0:T(8,128)(2,1)S(1)}, bf16[8,1,32,512]{3,2,1,0:T(8,128)(2,1)}, u32[]{:S(2)}) copy-start(bf16[8,1,32,512]{3,2,1,0:T(8,128)(2,1)} %copy.147) | copy-start | bytes 786436
  95.0 23.1 %copy-start.27 = (f32[32]{0:T(128)S(1)}, f32[32]{0:T(128)}, u32[]{:S(2)}) copy-start(f32[32]{0:T(128)} %param.17) | copy-start | bytes 388
  100.5 13.9 %copy-start.17 = (bf16[8,1,32,512]{3,2,1,0:T(8,128)(2,1)S(1)}, bf16[8,1,32,512]{3,2,1,0:T(8,128)(2,1)}, u32[]{:S(2)}) copy-start(bf16[8,1,32,512]{3,2,1,0:T(8,128)(2,1)} %copy.144) | copy-start | bytes 786436
  100.5 14.6 %copy-start.15 = (bf16[8,1,32,512]{3,2,1,0:T(8,128)(2,1)S(1)}, bf16[8,1,32,512]{3,2,1,0:T(8,128)(2,1)}, u32[]{:S(2)}) copy-start(bf16[8,1,32,512]{3,2,1,0:T(8,128)(2,1)} %copy.145) | copy-start | bytes 786436
  100.5 15.3 %copy-start.14 = (bf16[8,1,32,512]{3,2,1,0:T(8,128)(2,1)S(1)}, bf16[8,1,32,512]{3,2,1,0:T(8,128)(2,1)}, u32[]{:S(2)}) copy-start(bf16[8,1,32,512]{3,2,1,0:T(8,128)(2,1)} %copy.146) | copy-start | bytes 786436
  100.5 16.8 %copy-start.16 = (bf16[8,1,32,512]{3,2,1,0:T(8,128)(2,1)S(1)}, bf16[8,1,32,512]{3,2,1,0:T(8,128)(2,1)}, u32[]{:S(2)}) copy-start(bf16[8,1,32,512]{3,2,1,0:T(8,128)(2,1)} %copy.148) | copy-start | bytes 786436
  124.4 58.2 %copy-start.19 = (bf16[32,64]{1,0:T(8,128)(2,1)S(1)}, bf16[32,64]{1,0:T(8,128)(2,1)}, u32[]{:S(2)}) copy-start(bf16[32,64]{1,0:T(8,128)(2,1)} %param.18) | copy-start | bytes 12292
  124.4 58.2 %copy-start.28 = (f32[64]{0:T(128)S(1)}, f32[64]{0:T(128)}, u32[]{:S(2)}) copy-start(f32[64]{0:T(128)} %param.19) | copy-start | bytes 772
  148.4 35.0 %copy-start.29 = (f32[64,2]{0,1:T(2,128)S(1)}, f32[64,2]{0,1:T(2,128)}, u32[]{:S(2)}) copy-start(f32[64,2]{0,1:T(2,128)} %param.20) | copy-start | bytes 1540
  150.3 19.0 %all-to-all-start.1 = ((bf16[32,32,256]{2,0,1:T(8,128)(2,1)}), bf16[32,32,256]{2,0,1:T(8,128)(2,1)S(1)}, u32[]{:S(2)}, u32[]{:S(2)}) async-start(bf16[32,32,256]{2,0,1:T(8,128)(2,1)} %select_select_fusion), calls=%async_computation.1 | async-start | bytes 1048576 | tf_op jit(solution)/shard_map/all_to_all | solution.py:126
  157.7 48.9 %copy-start.26 = (f32[8]{0:T(128)}, f32[8]{0:T(128)S(1)}, u32[]{:S(2)}) copy-start(f32[8]{0:T(128)S(1)} %add_multiply_fusion.1) | copy-start | bytes 100
  157.8 60.7 %copy-start.21 = (s32[512]{0:T(512)S(1)}, s32[512]{0:T(512)}, u32[]{:S(2)}) copy-start(s32[512]{0:T(512)} %param.25) | copy-start | bytes 6148
  157.8 60.7 %copy-start.23 = (f32[512]{0:T(512)S(1)}, f32[512]{0:T(512)}, u32[]{:S(2)}) copy-start(f32[512]{0:T(512)} %param.24) | copy-start | bytes 6148
  157.8 60.7 %copy-start.24 = (f32[512]{0:T(512)S(1)}, f32[512]{0:T(512)}, u32[]{:S(2)}) copy-start(f32[512]{0:T(512)} %param.23) | copy-start | bytes 6148
  183.4 58.9 %copy-start.11 = (f32[64,4096]{1,0:T(8,128)}, f32[64,4096]{1,0:T(8,128)S(1)}, u32[]{:S(2)}) copy-start(f32[64,4096]{1,0:T(8,128)S(1)} %fusion) | copy-start | bytes 3145732
  218.4 1.2 copy-start.22
  218.5 1.2 copy-start.25
  219.7 0.9 copy-start.20
  263.1 95.2 %all-to-all-start.2 = ((f32[32,32,256]{2,0,1:T(8,128)}), f32[32,32,256]{2,0,1:T(8,128)S(1)}, u32[]{:S(2)}, u32[]{:S(2)}) async-start(f32[32,32,256]{2,0,1:T(8,128)} %copy.154), calls=%async_computation.2 | async-start | bytes 2097152 | tf_op jit(solution)/shard_map/all_to_all | solution.py:175
  281.7 373.3 %all-reduce.34.cloned.1.call-start = ((), (), s32[]{:S(2)}) async-start(), calls=%async_computation.3 | async-start | bytes 229376 | tf_op jit(solution)/shard_map/psum | solution.py:199
  358.2 48.5 %copy-start.10 = (f32[32,8,512]{2,0,1:T(8,128)S(1)}, f32[32,8,512]{2,0,1:T(8,128)}, u32[]{:S(2)}) copy-start(f32[32,8,512]{2,0,1:T(8,128)} %get-tuple-element.362) | copy-start | bytes 1572868
  497.9 16.8 %copy-start.2 = (f32[8,1,32,512]{2,3,0,1:T(8,128)S(1)}, f32[8,1,32,512]{2,3,0,1:T(8,128)}, u32[]{:S(2)}) copy-start(f32[8,1,32,512]{2,3,0,1:T(8,128)} %copy.223) | copy-start | bytes 1572868
  497.9 16.8 %copy-start.3 = (f32[8,1,32,512]{2,3,0,1:T(8,128)S(1)}, f32[8,1,32,512]{2,3,0,1:T(8,128)}, u32[]{:S(2)}) copy-start(f32[8,1,32,512]{2,3,0,1:T(8,128)} %copy.222) | copy-start | bytes 1572868
  497.9 16.8 %copy-start.4 = (f32[8,1,32,512]{2,3,0,1:T(8,128)S(1)}, f32[8,1,32,512]{2,3,0,1:T(8,128)}, u32[]{:S(2)}) copy-start(f32[8,1,32,512]{2,3,0,1:T(8,128)} %copy.221) | copy-start | bytes 1572868
  497.9 16.8 %copy-start.5 = (f32[8,1,32,512]{2,3,0,1:T(8,128)S(1)}, f32[8,1,32,512]{2,3,0,1:T(8,128)}, u32[]{:S(2)}) copy-start(f32[8,1,32,512]{2,3,0,1:T(8,128)} %copy.220) | copy-start | bytes 1572868
  497.9 16.8 %copy-start.6 = (f32[8,1,32,512]{2,3,0,1:T(8,128)S(1)}, f32[8,1,32,512]{2,3,0,1:T(8,128)}, u32[]{:S(2)}) copy-start(f32[8,1,32,512]{2,3,0,1:T(8,128)} %copy.219) | copy-start | bytes 1572868
  514.7 141.9 %copy-start.1 = (bf16[32,864]{1,0:T(8,128)(2,1)S(1)}, bf16[32,864]{1,0:T(8,128)(2,1)}, u32[]{:S(2)}) copy-start(bf16[32,864]{1,0:T(8,128)(2,1)} %param.16) | copy-start | bytes 165892
Sparse Core Ops, SparseCore 0:
  420.6 234.3 all-reduce.33
where the time goes:
time: 677 us; the launch traced here: 665 us
  local copies, waits for them, and re-layouts  249 us (37%)
  blocking collectives  192 us (28%)
  waiting for transfers between devices  76.9 us (11%)
  other arithmetic  70.1 us (10%)
  starting transfers between devices  34.7 us (5%)
  matrix products  25.1 us (4%)
  between operations  16.9 us (2%)
    unnamed x118, local copies, waits for them, and re-layouts  119 us
    psum x1, blocking collectives, local(): lax.psum((conv_grad, conv_bias_grad, grad_one, grad_bias_one, grad_two),...  72.8 us
    psum x1, blocking collectives, local(): loss_mean = lax.psum(ray_loss, 'sector') / (ray_count * sectors)  71.8 us
    psum x1, waiting for transfers between devices, local(): lax.psum((conv_grad, conv_bias_grad, grad_one, grad_bias_one, grad_two),...  65.3 us
    reshape x26, local copies, waits for them, and re-layouts, unfold_cells(): jnp.stack(columns, axis=1).reshape(brick_count, 27 * channel_width, 512)  51.4 us
    scatter-add x1, other arithmetic, local(): table_grad = jnp.zeros((channels, brick_count * 512), jnp.float32).at[:,...  45 us
    all_gather x2, blocking collectives, entering(): pieces = lax.all_gather(value, axis)  35.5 us
    gather x2, local copies, waits for them, and re-layouts, local(): picked = jnp.take(cell_table, jnp.where(live_slot, owner_addr, 0), axis=1)  25 us
  transfers between devices with their start and end apart: 4, of which 2 were waited for; matrix products, arithmetic and copies ran while one was open for 31% of the time, Pallas kernels for 0%

commit v1 on v0

--- a/solution.py
+++ b/solution.py
@@ -197,7 +197,7 @@
         conv_back, start, jnp.arange(group_total, dtype=jnp.int32)
     )
     summed = lax.psum(
-        (conv_grad, conv_bias_grad, grad_one, grad_bias_one, grad_two), ("shell", "sector")
+        lax.psum((conv_grad, conv_bias_grad, grad_one, grad_bias_one, grad_two), "shell"), "sector"
     )
     return (
         loss_mean,

time: 677 us -> 633 us (0.935)
  the two profiles are of different devices: /device:TPU:1 before, /device:TPU:0 now
where the time goes in v1:
time: 633 us; the launch traced here: 621 us
  local copies, waits for them, and re-layouts  248 us (39%)
  blocking collectives  213 us (34%)
  other arithmetic  75.5 us (12%)
  matrix products  25.1 us (4%)
  waiting for transfers between devices  23.9 us (4%)
  starting transfers between devices  17.6 us (3%)
  between operations  16.8 us (3%)
    psum x1, blocking collectives, local(): loss_mean = lax.psum(ray_loss, 'sector') / (ray_count * sectors)  124 us
    unnamed x108, local copies, waits for them, and re-layouts  117 us
    reshape x26, local copies, waits for them, and re-layouts, unfold_cells(): jnp.stack(columns, axis=1).reshape(brick_count, 27 * channel_width, 512)  51.4 us
    all_gather x2, blocking collectives, entering(): pieces = lax.all_gather(value, axis)  46.4 us
    scatter-add x1, other arithmetic, local(): table_grad = jnp.zeros((channels, brick_count * 512), jnp.float32).at[:,...  44.8 us
    psum x1, blocking collectives, local(): lax.psum((conv_grad, conv_bias_grad, grad_one, grad_bias_one, grad_two),...  27.7 us
    gather x2, local copies, waits for them, and re-layouts, local(): picked = jnp.take(cell_table, jnp.where(live_slot, owner_addr, 0), axis=1)  25 us
    add_any x1, other arithmetic, unfold_cells(): padded[:, :, a:a + 8, b:b + 8, c:c + 8]  18.2 us
  transfers between devices with their start and end apart: 5, of which 2 were waited for; matrix products, arithmetic and copies ran while one was open for 34% of the time, Pallas kernels for 0%

profile of v1, /device:TPU:0, one launch (start us, length us, event | category | flops | bytes accessed | tf_op | source)
XLA Modules:
  0.0 620.9 jit_solution(1811926216476882610)
XLA Ops:
  8.6 5.6 all-to-all-start
  15.6 3.4 pad_slice_fusion.1
  19.0 6.8 %pad_slice_fusion = (bf16[8,32,8,8,8]{1,4,3,2,0:T(8,128)(2,1)}, bf16[8,32,8,8,8]{1,4,3,2,0:T(8,128)(2,1)}, bf16[8,32,8,8,8]{1,4,3,2,0:T(8,128)(2,1)}, bf16[8,32,...) fusion(bf16[8,32,8,8,8]{1,4,3,2,0:T(8,128)(2,1)S(1)} %bitcast.139), kind=kLoop, calls=%fused_computation.8 | loop fusion | bytes 5242880 | tf_op jit(solution)/shard_map/while/body/eval_jaxpr/slice | solution.py:33
  115.1 5.1 multiply_convert_fusion
  121.4 24.0 %gather_fusion = bf16[8192,32]{1,0:T(8,128)(2,1)S(1)} fusion(bf16[32,4096]{0,1:T(8,128)(2,1)S(1)} %bitcast.136, s32[8192]{0:T(1024)S(1)} %broadcast_clamp_fusion), kind=kCustom, calls=%fused_computation | custom fusion | bytes 1081344 | tf_op jit(solution)/shard_map/jit(_take)/gather | solution.py:123
  147.4 7.4 %all-to-all-start.1 = ((bf16[32,32,256]{2,0,1:T(8,128)(2,1)}), bf16[32,32,256]{2,0,1:T(8,128)(2,1)S(1)}, u32[]{:S(2)}, u32[]{:S(2)}) async-start(bf16[32,32,256]{2,0,1:T(8,128)(2,1)} %select_select_fusion), calls=%async_computation.1 | async-start | bytes 1048576 | tf_op jit(solution)/shard_map/all_to_all | solution.py:126
  154.9 11.1 %all-to-all-done.1 = bf16[32,32,256]{2,0,1:T(8,128)(2,1)S(1)} async-done(((bf16[32,32,256]{2,0,1:T(8,128)(2,1)}), bf16[32,32,256]{2,0,1:T(8,128)(2,1)S(1)}, u32[]{:S(2)}, u32[]{:S(2)}) %all-to-all-start.1) | async-done | bytes 524320 | tf_op jit(solution)/shard_map/all_to_all | solution.py:126
  167.0 12.1 %gather_fusion.1 = bf16[4096,32]{1,0:T(8,128)(2,1)S(1)} fusion(bf16[32,8192]{0,1:T(8,128)(2,1)S(1)} %bitcast.163, s32[4096]{0:T(1024)S(1)} %broadcast_clamp_fusion.1), kind=kCustom, calls=%fused_computation.1 | custom fusion | bytes 540672 | tf_op jit(solution)/shard_map/jit(_take)/gather | solution.py:133
  183.6 25.4 %all-gather.2 = f32[8,1,512]{2,1,0:T(1,128)S(1)} all-gather(f32[1,1,512]{2,1,0:T(1,128)S(1)} %bitcast.209), channel_id=2, replica_groups=mesh['shell'=8,'sector'=32] {'shell'}, dimensions={0}, use_global_device_ids=true | all-gather | bytes 18432 | tf_op jit(solution)/shard_map/all_gather | solution.py:14
  209.4 15.7 %all-reduce.32 = (f32[512]{0:T(512)S(1)}, f32[512]{0:T(512)S(1)}, f32[512]{0:T(512)S(1)}) all-reduce(f32[512]{0:T(512)S(1)} %get-tuple-element.265, f32[512]{0:T(512)S(1)} %get-tuple-element.365, f32[512]{0:T(512)S(1)} %get-tuple-element.364), channel_id=1, replica_groups=mesh['shell'=8,'sector'=32] {'shell'}, use_global_device_ids=true, to_apply=%region_8.9 | all-reduce | flops 1536 | bytes 12288 | tf_op jit(solution)/shard_map/psum | solution.py:154
  227.4 21.0 %all-gather.3 = f32[8,1,512]{2,1,0:T(1,128)S(1)} all-gather(f32[1,1,512]{2,1,0:T(1,128)} %bitcast.210), channel_id=3, replica_groups=mesh['shell'=8,'sector'=32] {'shell'}, dimensions={0}, use_global_device_ids=true | all-gather | bytes 18432 | tf_op jit(solution)/shard_map/all_gather | solution.py:14
  254.0 4.0 fusion.57
  257.9 13.2 %scatter_custom_fusion = f32[32,8192]{0,1:T(8,128)} fusion(s32[4096]{0:T(1024)S(1)} %bitcast.205, f32[4096,32]{1,0:T(8,128)} %fusion.57, f32[]{:T(128)} %constant.164.clone.1), kind=kCustom, calls=%fused_computation.45 | custom fusion | bytes 1049088 | tf_op jit(solution)/shard_map/scatter | solution.py:174
  271.1 3.6 copy.154
  274.7 4.3 all-to-all-start.2
  283.0 12.8 %all-to-all-done.2 = f32[32,32,256]{2,0,1:T(8,128)S(1)} async-done(((f32[32,32,256]{2,0,1:T(8,128)}), f32[32,32,256]{2,0,1:T(8,128)S(1)}, u32[]{:S(2)}, u32[]{:S(2)}) %all-to-all-start.2) | async-done | bytes 1048608 | tf_op jit(solution)/shard_map/all_to_all | solution.py:175
  295.9 2.8 copy.156
  298.7 44.8 %scatter_custom_fusion.1 = f32[32,4096]{0,1:T(8,128)S(1)} fusion(s32[8192]{0:T(1024)} %bitcast.208, f32[8192,32]{1,0:T(8,128)} %copy.156, f32[]{:T(128)} %constant.164.clone.1), kind=kCustom, calls=%fused_computation.58 | custom fusion | flops 262144 | bytes 524800 | tf_op jit(solution)/shard_map/scatter-add | solution.py:186
  344.5 5.8 convolution_bitcast_fusion.2
  354.2 3.6 fusion.54
  359.8 3.0 copy.197
  362.8 3.0 copy.204
  365.8 3.0 copy.203
  368.8 3.0 copy.202
  371.8 3.0 copy.201
  374.8 3.0 copy.200
  377.8 2.9 copy.199
  380.7 3.0 copy.218
  383.7 3.0 copy.217
  386.7 3.0 copy.216
  389.8 3.0 copy.215
  392.8 3.0 copy.214
  395.7 3.0 copy.213
  398.7 2.9 copy.212
  401.6 3.0 copy.211
  404.7 3.0 copy.210
  407.6 3.0 copy.209
  410.7 3.0 copy.208
  413.7 3.0 copy.207
  416.6 3.0 copy.206
  419.6 3.0 copy.205
  422.6 18.2 %pad_add_fusion = f32[8,32,10,10,10]{1,4,3,2,0:T(8,128)} fusion(f32[8,32,8,8,8]{1,4,3,2,0:T(8,128)} %bitcast.148, f32[8,32,8,8,8]{1,4,3,2,0:T(8,128)} %bitcast.149, f32[8,32,8,8,8]{1,4,3,2,0:T(8,128)} %bitcast.150, f32[8,32,8,8,8]{1,4,3,2,0:T(8,128)} %bitcast.151, f32[8,32,8,8,8]{1,4,3,2,0:T(8,128)} %bitcast.152, f32[8,32,8,8,8]{1,4,3,2,0:T(8,128)} %bitcast.153, ...), kind=kLoop, calls=%fused_computation.34 | loop fusion | flops 5376000 | bytes 12558336 | tf_op jit(solution)/shard_map/while/body/eval_jaxpr/transpose(jvp())/add_any | solution.py:33
  441.4 3.0 copy.222
  444.4 3.0 copy.221
  447.5 3.0 copy.220
  452.4 5.3 fusion.1
  457.7 27.7 %all-reduce.31 = (f32[32]{0:T(128)S(1)}, f32[32,64]{1,0:T(8,128)S(1)}, f32[64]{0:T(128)S(1)}, f32[64,2]{0,1:T(2,128)S(1)}) all-reduce(f32[32]{0:T(128)S(1)} %get-tuple-element.294, f32[32,64]{1,0:T(8,128)S(1)} %fusion.21, f32[64]{0:T(128)S(1)} %get-tuple-element.368, ...), channel_id=1, replica_groups=mesh['shell'=8,'sector'=32] {'shell'}, use_global_device_ids=true, to_apply=%region_19.20 | all-reduce | flops 2272 | bytes 18176 | tf_op jit(solution)/shard_map/psum | solution.py:200
  485.4 123.8 %all-reduce.30 = (f32[]{:T(128)}, f32[32]{0:T(128)}, f32[32,64]{1,0:T(8,128)}, f32[64]{0:T(128)}, f32[64,2]{0,1:T(2,128)}) all-reduce(f32[]{:T(128)} %get-tuple-element.359, f32[32]{0:T(128)S(1)} %get-tuple-element.287, f32[32,64]{1,0:T(8,128)S(1)} %get-tuple-element.288, ...), channel_id=1, replica_groups=mesh['shell'=8,'sector'=32] {'sector'}, use_global_device_ids=true, to_apply=%region_10.11 | all-reduce | flops 2273 | bytes 18184 | tf_op jit(solution)/shard_map/psum | solution.py:170
  (193 shorter events, 125.2 us)
Async XLA Ops:
  7.2 107.9 %copy-start = (bf16[32,864]{1,0:T(8,128)(2,1)S(1)}, bf16[32,864]{1,0:T(8,128)(2,1)}, u32[]{:S(2)}) copy-start(bf16[32,864]{1,0:T(8,128)(2,1)} %param.16) | copy-start | bytes 165892
  8.6 112.1 %all-to-all-start = ((s32[32,1,256]{2,1,0:T(1,128)}), s32[32,1,256]{2,1,0:T(1,128)S(1)}, u32[]{:S(2)}, u32[]{:S(2)}) async-start(s32[32,1,256]{2,1,0:T(1,128)} %all_to_all.12), calls=%async_computation | async-start | bytes 65536 | tf_op jit(solution)/shard_map/all_to_all | solution.py:119
  19.0 6.9 %copy-start.13 = (s32[1,4096]{1,0:T(1,128)S(1)}, s32[1,4096]{1,0:T(1,128)}, u32[]{:S(2)}) copy-start(s32[1,4096]{1,0:T(1,128)} %param.22) | copy-start | bytes 49156
  25.9 13.6 %copy-start.4 = (bf16[8,32,8,8,8]{1,4,3,2,0:T(8,128)(2,1)S(1)}, bf16[8,32,8,8,8]{1,4,3,2,0:T(8,128)(2,1)}, u32[]{:S(2)}) copy-start(bf16[8,32,8,8,8]{1,4,3,2,0:T(8,128)(2,1)} %get-tuple-element.350) | copy-start | bytes 786436
  40.6 22.6 %copy-start.3 = (bf16[8,32,8,8,8]{1,4,3,2,0:T(8,128)(2,1)S(1)}, bf16[8,32,8,8,8]{1,4,3,2,0:T(8,128)(2,1)}, u32[]{:S(2)}) copy-start(bf16[8,32,8,8,8]{1,4,3,2,0:T(8,128)(2,1)} %get-tuple-element.335) | copy-start | bytes 786436
  58.6 30.3 %copy-start.7 = (bf16[1,8,32,512]{3,2,1,0:T(8,128)(2,1)S(1)}, bf16[1,8,32,512]{3,2,1,0:T(8,128)(2,1)}, u32[]{:S(2)}) copy-start(bf16[1,8,32,512]{3,2,1,0:T(8,128)(2,1)} %param.15) | copy-start | bytes 786436
  64.2 32.3 %copy-start.2 = (bf16[8,32,8,8,8]{1,4,3,2,0:T(8,128)(2,1)S(1)}, bf16[8,32,8,8,8]{1,4,3,2,0:T(8,128)(2,1)}, u32[]{:S(2)}) copy-start(bf16[8,32,8,8,8]{1,4,3,2,0:T(8,128)(2,1)} %get-tuple-element.341) | copy-start | bytes 786436
  89.7 23.9 %copy-start.8 = (bf16[8,1,32,512]{3,2,1,0:T(8,128)(2,1)S(1)}, bf16[8,1,32,512]{3,2,1,0:T(8,128)(2,1)}, u32[]{:S(2)}) copy-start(bf16[8,1,32,512]{3,2,1,0:T(8,128)(2,1)} %copy.147) | copy-start | bytes 786436
  92.0 23.1 %copy-start.22 = (f32[32]{0:T(128)S(1)}, f32[32]{0:T(128)}, u32[]{:S(2)}) copy-start(f32[32]{0:T(128)} %param.17) | copy-start | bytes 388
  97.6 13.8 %copy-start.12 = (bf16[8,1,32,512]{3,2,1,0:T(8,128)(2,1)S(1)}, bf16[8,1,32,512]{3,2,1,0:T(8,128)(2,1)}, u32[]{:S(2)}) copy-start(bf16[8,1,32,512]{3,2,1,0:T(8,128)(2,1)} %copy.144) | copy-start | bytes 786436
  97.6 14.6 %copy-start.10 = (bf16[8,1,32,512]{3,2,1,0:T(8,128)(2,1)S(1)}, bf16[8,1,32,512]{3,2,1,0:T(8,128)(2,1)}, u32[]{:S(2)}) copy-start(bf16[8,1,32,512]{3,2,1,0:T(8,128)(2,1)} %copy.145) | copy-start | bytes 786436
  97.6 15.3 %copy-start.9 = (bf16[8,1,32,512]{3,2,1,0:T(8,128)(2,1)S(1)}, bf16[8,1,32,512]{3,2,1,0:T(8,128)(2,1)}, u32[]{:S(2)}) copy-start(bf16[8,1,32,512]{3,2,1,0:T(8,128)(2,1)} %copy.146) | copy-start | bytes 786436
  97.6 16.8 %copy-start.11 = (bf16[8,1,32,512]{3,2,1,0:T(8,128)(2,1)S(1)}, bf16[8,1,32,512]{3,2,1,0:T(8,128)(2,1)}, u32[]{:S(2)}) copy-start(bf16[8,1,32,512]{3,2,1,0:T(8,128)(2,1)} %copy.148) | copy-start | bytes 786436
  121.4 57.7 %copy-start.14 = (bf16[32,64]{1,0:T(8,128)(2,1)S(1)}, bf16[32,64]{1,0:T(8,128)(2,1)}, u32[]{:S(2)}) copy-start(bf16[32,64]{1,0:T(8,128)(2,1)} %param.18) | copy-start | bytes 12292
  121.4 57.7 %copy-start.23 = (f32[64]{0:T(128)S(1)}, f32[64]{0:T(128)}, u32[]{:S(2)}) copy-start(f32[64]{0:T(128)} %param.19) | copy-start | bytes 772
  145.5 34.5 %copy-start.24 = (f32[64,2]{0,1:T(2,128)S(1)}, f32[64,2]{0,1:T(2,128)}, u32[]{:S(2)}) copy-start(f32[64,2]{0,1:T(2,128)} %param.20) | copy-start | bytes 1540
  147.4 18.6 %all-to-all-start.1 = ((bf16[32,32,256]{2,0,1:T(8,128)(2,1)}), bf16[32,32,256]{2,0,1:T(8,128)(2,1)S(1)}, u32[]{:S(2)}, u32[]{:S(2)}) async-start(bf16[32,32,256]{2,0,1:T(8,128)(2,1)} %select_select_fusion), calls=%async_computation.1 | async-start | bytes 1048576 | tf_op jit(solution)/shard_map/all_to_all | solution.py:126
  154.8 54.2 %copy-start.21 = (f32[8]{0:T(128)}, f32[8]{0:T(128)S(1)}, u32[]{:S(2)}) copy-start(f32[8]{0:T(128)S(1)} %add_multiply_fusion.1) | copy-start | bytes 100
  154.8 70.2 %copy-start.16 = (s32[512]{0:T(512)S(1)}, s32[512]{0:T(512)}, u32[]{:S(2)}) copy-start(s32[512]{0:T(512)} %param.25) | copy-start | bytes 6148
  154.8 70.2 %copy-start.18 = (f32[512]{0:T(512)S(1)}, f32[512]{0:T(512)}, u32[]{:S(2)}) copy-start(f32[512]{0:T(512)} %param.24) | copy-start | bytes 6148
  154.8 70.2 %copy-start.19 = (f32[512]{0:T(512)S(1)}, f32[512]{0:T(512)}, u32[]{:S(2)}) copy-start(f32[512]{0:T(512)} %param.23) | copy-start | bytes 6148
  180.0 74.0 %copy-start.6 = (f32[64,4096]{1,0:T(8,128)}, f32[64,4096]{1,0:T(8,128)S(1)}, u32[]{:S(2)}) copy-start(f32[64,4096]{1,0:T(8,128)S(1)} %fusion) | copy-start | bytes 3145732
  225.0 1.2 copy-start.17
  225.1 1.2 copy-start.20
  226.3 0.9 copy-start.15
  274.7 21.1 %all-to-all-start.2 = ((f32[32,32,256]{2,0,1:T(8,128)}), f32[32,32,256]{2,0,1:T(8,128)S(1)}, u32[]{:S(2)}, u32[]{:S(2)}) async-start(f32[32,32,256]{2,0,1:T(8,128)} %copy.154), calls=%async_computation.2 | async-start | bytes 2097152 | tf_op jit(solution)/shard_map/all_to_all | solution.py:175
  279.0 173.4 %all-reduce.36.cloned.1.call-start = ((), (), s32[]{:S(2)}) async-start(), calls=%async_computation.3 | async-start | bytes 229376 | tf_op jit(solution)/shard_map/psum | solution.py:200
  283.0 61.0 %copy-start.5 = (f32[32,8,512]{2,0,1:T(8,128)S(1)}, f32[32,8,512]{2,0,1:T(8,128)}, u32[]{:S(2)}) copy-start(f32[32,8,512]{2,0,1:T(8,128)} %get-tuple-element.367) | copy-start | bytes 1572868
  357.8 253.1 %all-reduce.38.cloned.1.call-start = ((), (), s32[]{:S(2)}) async-start(), calls=%async_computation.4 | async-start | bytes 229376 | tf_op jit(solution)/shard_map/psum | solution.py:199
  452.4 160.1 %copy-start.1 = (bf16[32,864]{1,0:T(8,128)(2,1)S(1)}, bf16[32,864]{1,0:T(8,128)(2,1)}, u32[]{:S(2)}) copy-start(bf16[32,864]{1,0:T(8,128)(2,1)} %param.16) | copy-start | bytes 165892
Sparse Core Ops, SparseCore 0:
  357.9 67.7 all-reduce.35
  452.5 104.9 all-reduce.37
